TPU v7x, 128 devices: a whole 4x4x4 slice. The times are simulated.
128 devices in a mesh: group: 4 (over z), shard: 32 (over x, y, core).
Axes of the slice: x: 4, y: 4, z: 4, core: 2. Of those that a mesh axis runs over, the one named last changes fastest.
Arguments:
- vectors: float32 [16384, 256], P(('group', 'shard')), may hold values from -160 to 160
- item_codes: int32 [16384], P(('group', 'shard')), may hold values from 0 to 63, as said below
- coarse_book: float32 [64, 256], replicated, may hold values from -24 to 24
- fine_books: float32 [8, 16384, 256], P('group', 'shard'), may hold values from -2 to 2
Outputs:
- item_grad: float32 [16384, 256], P(('group', 'shard'))
- fine_grad: float32 [8, 16384, 256], P('group', 'shard')
- coarse_grad: float32 [64, 256], replicated
Inputs may be any that keep to these rules, and one draw needn't show every extreme that they name: `item_codes`: the items of one device fall into one group at most 32 times, and one group receives exactly 32 items from every device.
All inputs are finite; a program needn't handle non-finite values.
Results may differ from a plain program's by a relative error of at most 0.0003.
Values sent between devices are 32-bit elements; how exact they have to be, the bound alone decides.
No kernel may reach another device: no remote copies, remote signals or barrier semaphores. Data moves between devices by JAX's collectives and lax.ppermute only.
A program may use at most 192 MiB of HBM per device.

v0:
```python
import jax
import jax.numpy as jnp
from jax import lax
from jax.sharding import PartitionSpec as P

sharpness = 2.5
highest = lax.Precision.HIGHEST


def contract(former, latter, former_dim, latter_dim):
    return lax.dot_general(
        former,
        latter,
        (((former_dim,), (latter_dim,)), ((), ())),
        precision=highest,
        preferred_element_type=jnp.float32,
    )


def per_device(vectors, item_codes, coarse_book, fine_books):
    local_groups, book_rows, feature_count = fine_books.shape
    group_count = lax.axis_size("group")
    total_groups = local_groups * group_count
    coarse_total = coarse_book.shape[0]
    per_group = coarse_total // total_groups
    item_count = vectors.shape[0]
    slot_size = item_count // 4
    slot_total = local_groups * group_count * slot_size
    onehot = (item_codes[:, None] == jnp.arange(coarse_total, dtype=jnp.int32)[None, :]).astype(
        jnp.float32
    )
    residual = vectors - contract(onehot, coarse_book, 1, 0)
    group_of = item_codes // per_group
    member = (group_of[:, None] == jnp.arange(total_groups, dtype=jnp.int32)[None, :]).astype(
        jnp.int32
    )
    position = jnp.sum((jnp.cumsum(member, axis=0) - 1) * member, axis=1)
    target = (
        group_of % local_groups * group_count + group_of // local_groups
    ) * slot_size + position
    placing = (jnp.arange(slot_total, dtype=jnp.int32)[:, None] == target[None, :]).astype(
        jnp.float32
    )
    outgoing = contract(placing, residual, 1, 0).reshape(
        local_groups, group_count, slot_size, feature_count
    )
    occupied = jnp.sum(placing, axis=1).reshape(local_groups, group_count, slot_size)
    arrived, arrived_mask = (
        lax.all_to_all(outgoing, "group", split_axis=1, concat_axis=1, tiled=True),
        lax.all_to_all(occupied, "group", split_axis=1, concat_axis=1, tiled=True),
    )
    own_count = group_count * slot_size
    own_rows = arrived.reshape(local_groups, own_count, feature_count)
    own_live = arrived_mask.reshape(local_groups, own_count)
    row_grads = []
    book_grads = []
    spread_rows, spread_mask = (
        lax.all_gather(arrived, "shard", axis=1, tiled=True),
        lax.all_gather(arrived_mask, "shard", axis=1, tiled=True),
    )
    row_total = spread_rows.shape[1] * slot_size
    all_rows = spread_rows.reshape(local_groups, row_total, feature_count)
    for book_index in range(local_groups):
        codebook = fine_books[book_index]
        entries = all_rows[book_index]
        scores = sharpness * contract(entries, codebook, 1, 1)
        peak_score = lax.pmax(jnp.max(scores, axis=1), "shard")
        weights = jnp.exp(scores - peak_score[:, None])
        partial_total = jnp.sum(weights, axis=1)
        partial_quant = contract(weights, codebook, 1, 0)
        quant_sum, denominator_own = (
            lax.psum_scatter(partial_quant, "shard", scatter_dimension=0, tiled=True),
            lax.psum_scatter(partial_total, "shard", scatter_dimension=0, tiled=True),
        )
        quantized = quant_sum / denominator_own[:, None]
        own_error = (quantized - own_rows[book_index]) * own_live[book_index][:, None]
        own_inner = jnp.sum(own_error * quantized, axis=1)
        error_rows, inner_term, denominator = (
            lax.all_gather(own_error, "shard", axis=0, tiled=True),
            lax.all_gather(own_inner, "shard", axis=0, tiled=True),
            lax.all_gather(denominator_own, "shard", axis=0, tiled=True),
        )
        probability = weights / denominator[:, None]
        alignment = contract(error_rows, codebook, 1, 1)
        slopes = probability * (alignment - inner_term[:, None])
        pushed = sharpness * contract(slopes, codebook, 1, 0)
        back_sum = lax.psum_scatter(pushed, "shard", scatter_dimension=0, tiled=True)
        row_grads.append(back_sum - own_error)
        book_grads.append(
            contract(probability, error_rows, 0, 0) + sharpness * contract(slopes, entries, 0, 0)
        )
    fine_grad = jnp.stack(book_grads)
    returned = jnp.stack(row_grads).reshape(local_groups, group_count, slot_size, feature_count)
    homeward = lax.all_to_all(returned, "group", split_axis=1, concat_axis=1, tiled=True)
    item_grad = contract(placing, homeward.reshape(slot_total, feature_count), 0, 0)
    coarse_grad = lax.psum(-contract(onehot, item_grad, 0, 0), ("group", "shard"))
    return (item_grad, fine_grad, coarse_grad)


def solution(mesh):
    placed = (P(("group", "shard"), None), P(("group", "shard")), P(), P("group", "shard", None))
    return jax.shard_map(
        per_device,
        mesh=mesh,
        in_specs=placed,
        out_specs=(P(("group", "shard"), None), P("group", "shard", None), P()),
        check_vma=False,
    )
```

profile of v0, /device:TPU:1, one launch (start us, length us, event | category | flops | bytes accessed | tf_op | source)
XLA Modules:
  0.0 839.6 jit_solution(5621896040765602508)
XLA Ops:
  10.5 11.3 %all_to_all.15 = f32[2,4,32,256]{3,2,0,1:T(8,128)} all-to-all(f32[2,4,32,256]{3,2,0,1:T(8,128)S(1)} %copy.28), channel_id=1, replica_groups=mesh['group'=4,'shard'=32] {'group'}, dimensions={1} | all-to-all | bytes 524288 | tf_op jit(solution)/shard_map/all_to_all | solution.py:49
  21.9 54.1 %all-gather.8.cloned.1.call-done = f32[2,128,32,256]{3,2,0,1:T(8,128)} async-done(((f32[2,4,32,256]{3,2,0,1:T(8,128)}), f32[2,128,32,256]{3,2,0,1:T(8,128)}) %all-gather.8.cloned.1.call-update) | async-done | bytes 8388624 | tf_op jit(solution)/shard_map/all_gather | solution.py:58
  76.0 4.4 fusion.61
  80.4 9.2 %multiply_reduce_fusion = (f32[4096]{0:T(1024)S(1)}, f32[4096,512]{0,1:T(8,128)}) fusion(f32[4096,256]{1,0:T(8,128)S(1)} %bitcast.75, f32[2,512,256]{2,1,0:T(8,128)S(1)} %copy-done.8), kind=kOutput, calls=%fused_computation.4 | convolution fusion | flops 6446641152 | bytes 13123584 | tf_op jit(solution)/shard_map/dot_general | solution.py:11
  89.6 9.2 %multiply_reduce_fusion.1 = (f32[4096]{0:T(1024)S(1)}, f32[4096,512]{0,1:T(8,128)}) fusion(f32[4096,256]{1,0:T(8,128)S(1)} %bitcast.77, f32[2,512,256]{2,1,0:T(8,128)S(1)} %copy-done.8), kind=kOutput, calls=%fused_computation.5 | convolution fusion | flops 6446641152 | bytes 13123584 | tf_op jit(solution)/shard_map/dot_general | solution.py:11
  98.8 121.4 %all-reduce.3 = (f32[4096]{0:T(1024)S(1)}, f32[4096]{0:T(1024)S(1)}) all-reduce(f32[4096]{0:T(1024)S(1)} %get-tuple-element.17, f32[4096]{0:T(1024)S(1)} %get-tuple-element.19), channel_id=1, replica_groups=mesh['group'=4,'shard'=32] {'shard'}, use_global_device_ids=true, to_apply=%region_11.12 | all-reduce | flops 8192 | bytes 65536 | tf_op jit(solution)/shard_map/pmax | solution.py:67
  220.2 17.2 %fusion = f32[4096,256]{1,0:T(8,128)} fusion(f32[4096,512]{0,1:T(8,128)} %get-tuple-element.20, f32[4096]{0:T(1024)S(1)} %get-tuple-element.8, f32[2,512,256]{2,1,0:T(8,128)S(1)} %copy-done.8), kind=kOutput, calls=%fused_computation.8 | convolution fusion | flops 6446645248 | bytes 13123584 | tf_op jit(solution)/shard_map/dot_general | solution.py:11
  237.9 17.2 %fusion.3 = f32[4096,256]{1,0:T(8,128)} fusion(f32[4096,512]{0,1:T(8,128)} %get-tuple-element.18, f32[4096]{0:T(1024)S(1)} %get-tuple-element.7, f32[2,512,256]{2,1,0:T(8,128)S(1)} %copy-done.8), kind=kOutput, calls=%fused_computation.11 | convolution fusion | flops 6446645248 | bytes 13123584 | tf_op jit(solution)/shard_map/dot_general | solution.py:11
  255.9 4.1 all-to-all-start.1
  261.3 2.9 all-to-all-done.1
  264.3 5.0 fusion.2
  269.3 5.0 fusion.5
  274.3 125.8 %all-reduce.2 = (f32[4096]{0:T(1024)S(1)}, f32[4096]{0:T(1024)S(1)}) all-reduce(f32[4096]{0:T(1024)S(1)} %fusion.5, f32[4096]{0:T(1024)S(1)} %fusion.2), channel_id=5, replica_groups=mesh['group'=4,'shard'=32] {'shard'}, use_global_device_ids=true, to_apply=%region_13.14.clone | all-reduce | flops 8192 | bytes 65536
  406.7 22.7 %all-gather = f32[32,1,128]{2,1,0:T(1,128)S(1)} all-gather(f32[1,1,128]{2,1,0:T(1,128)S(1)} %dynamic-slice_bitcast_fusion), channel_id=1, replica_groups=mesh['group'=4,'shard'=32] {'shard'}, dimensions={0}, use_global_device_ids=true | all-gather | bytes 16896 | tf_op jit(solution)/shard_map/all_gather | solution.py:81
  429.4 20.5 %all-gather.1 = f32[32,1,128]{2,1,0:T(1,128)S(1)} all-gather(f32[1,1,128]{2,1,0:T(1,128)S(1)} %bitcast.89), channel_id=1, replica_groups=mesh['group'=4,'shard'=32] {'shard'}, dimensions={0}, use_global_device_ids=true | all-gather | bytes 16896 | tf_op jit(solution)/shard_map/all_gather | solution.py:80
  449.9 5.1 all-gather.10.cloned.1.call-done
  455.0 12.0 %subtract_multiply_fusion.1 = f32[4096,512]{0,1:T(8,128)S(1)} fusion(f32[4096,256]{1,0:T(8,128)} %all-gather.10.cloned.1.call-done, f32[4096]{0:T(1024)S(1)} %bitcast.87, f32[4096]{0:T(1024)S(1)} %bitcast.85, f32[4096]{0:T(1024)S(1)} %get-tuple-element.8, f32[4096,512]{0,1:T(8,128)} %get-tuple-element.20, f32[2,512,256]{2,1,0:T(8,128)S(1)} %copy-done.8), kind=kOutput, calls=%fused_computation.2 | convolution fusion | flops 6452936704 | bytes 21544960 | tf_op jit(solution)/shard_map/dot_general | solution.py:11
  467.0 3.2 copy-done.2
  470.3 15.4 %convolution_multiply_fusion.1 = f32[4096,256]{1,0:T(8,128)} fusion(f32[4096,512]{0,1:T(8,128)S(1)} %subtract_multiply_fusion.1, f32[2,512,256]{2,1,0:T(8,128)S(1)} %copy-done.8), kind=kOutput, calls=%fused_computation.7 | convolution fusion | flops 6443499520 | bytes 13107200 | tf_op jit(solution)/shard_map/dot_general | solution.py:11
  485.9 20.7 %all-gather.2 = f32[32,1,128]{2,1,0:T(1,128)S(1)} all-gather(f32[1,1,128]{2,1,0:T(1,128)S(1)} %dynamic-slice_bitcast_fusion.1), channel_id=1, replica_groups=mesh['group'=4,'shard'=32] {'shard'}, dimensions={0}, use_global_device_ids=true | all-gather | bytes 16896 | tf_op jit(solution)/shard_map/all_gather | solution.py:81
  506.5 20.0 %all-gather.3 = f32[32,1,128]{2,1,0:T(1,128)S(1)} all-gather(f32[1,1,128]{2,1,0:T(1,128)S(1)} %bitcast.90), channel_id=1, replica_groups=mesh['group'=4,'shard'=32] {'shard'}, dimensions={0}, use_global_device_ids=true | all-gather | bytes 16896 | tf_op jit(solution)/shard_map/all_gather | solution.py:80
  526.5 12.2 %subtract_multiply_fusion = f32[4096,512]{0,1:T(8,128)S(1)} fusion(f32[4096,256]{1,0:T(8,128)} %all-gather.12.cloned.1.call-done, f32[4096]{0:T(1024)S(1)} %bitcast.88, f32[4096]{0:T(1024)S(1)} %bitcast.83, f32[4096]{0:T(1024)S(1)} %get-tuple-element.7, f32[4096,512]{0,1:T(8,128)} %get-tuple-element.18, f32[2,512,256]{2,1,0:T(8,128)S(1)} %copy-done.8), kind=kOutput, calls=%fused_computation | convolution fusion | flops 6452936704 | bytes 21544960 | tf_op jit(solution)/shard_map/dot_general | solution.py:11
  538.7 3.2 copy-done.3
  541.9 15.4 %convolution_multiply_fusion = f32[4096,256]{1,0:T(8,128)} fusion(f32[4096,512]{0,1:T(8,128)S(1)} %subtract_multiply_fusion, f32[2,512,256]{2,1,0:T(8,128)S(1)} %copy-done.8), kind=kOutput, calls=%fused_computation.6 | convolution fusion | flops 6443499520 | bytes 13107200 | tf_op jit(solution)/shard_map/dot_general | solution.py:11
  557.3 10.2 %convolution_multiply_fusion.3 = f32[512,256]{1,0:T(8,128)S(1)} fusion(f32[4096,512]{0,1:T(8,128)} %copy-done.2, f32[4096,256]{1,0:T(8,128)} %bitcast.78), kind=kOutput, calls=%fused_computation.21 | convolution fusion | flops 6442582016 | bytes 13107200 | tf_op jit(solution)/shard_map/dot_general | solution.py:11
  567.6 6.7 convolution_multiply_fusion.2
  574.4 8.0 fusion.17
  582.4 3.7 reduce-scatter.7.cloned.1.call-done
  587.0 84.4 %reduce-scatter.11.cloned.1.call-done = f32[128,256]{1,0:T(8,128)} async-done(((f32[4096,256]{1,0:T(8,128)}), f32[128,256]{1,0:T(8,128)}) %reduce-scatter.11.cloned.1.call-update) | async-done | bytes 131088 | tf_op jit(solution)/shard_map/reduce_scatter | solution.py:87
  673.1 4.1 all-to-all-start.2
  677.2 10.9 %fusion.23 = f32[1,512,256]{2,1,0:T(8,128)S(1)} fusion(f32[512,256]{1,0:T(8,128)S(1)} %convolution_multiply_fusion.2, f32[4096,256]{1,0:T(8,128)} %all-gather.12.cloned.1.call-done, f32[4096,512]{0,1:T(8,128)} %get-tuple-element.18, f32[4096]{0:T(1024)S(1)} %bitcast.84, f32[4096]{0:T(1024)S(1)} %get-tuple-element.7), kind=kOutput, calls=%fused_computation.25 | convolution fusion | flops 6448873472 | bytes 13664256 | tf_op jit(solution)/shard_map/dot_general | solution.py:11
  690.5 140.6 %all-reduce.6.cloned.1.call-done = f32[64,256]{1,0:T(8,128)} async-done(((f32[64,256]{1,0:T(8,128)}), f32[64,256]{1,0:T(8,128)}) %all-reduce.6.cloned.1.call-update) | async-done | bytes 65552 | tf_op jit(solution)/shard_map/psum | solution.py:96
  (85 shorter events, 18.5 us)
Async XLA Ops:
  7.2 1.9 copy-start
  7.2 68.8 %all-gather.8.cloned.1.call-start = ((), (), s32[]{:S(2)}) async-start(), calls=%async_computation.7 | async-start | bytes 8650752 | tf_op jit(solution)/shard_map/all_gather | solution.py:58
  21.8 58.5 %copy-start.8 = (f32[2,512,256]{2,1,0:T(8,128)S(1)}, f32[2,512,256]{2,1,0:T(8,128)}, u32[]{:S(2)}) copy-start(f32[2,512,256]{2,1,0:T(8,128)} %param.7) | copy-start | bytes 3145732
  21.9 378.3 %reduce-scatter.5.cloned.1.call-start = ((), (), s32[]{:S(2)}) async-start(), calls=%async_computation.8 | async-start | bytes 4325376 | tf_op jit(solution)/shard_map/reduce_scatter | solution.py:72
  80.3 9.3 %copy-start.5 = (f32[1,128,32,256]{3,2,0,1:T(8,128)}, f32[1,128,32,256]{3,2,0,1:T(8,128)S(1)}, u32[]{:S(2)}) copy-start(f32[1,128,32,256]{3,2,0,1:T(8,128)S(1)} %get-tuple-element.14) | copy-start | bytes 12582916
  80.3 9.3 %copy-start.7 = (f32[1,128,32,256]{3,2,0,1:T(8,128)}, f32[1,128,32,256]{3,2,0,1:T(8,128)S(1)}, u32[]{:S(2)}) copy-start(f32[1,128,32,256]{3,2,0,1:T(8,128)S(1)} %get-tuple-element.13) | copy-start | bytes 12582916
  237.4 167.5 %reduce-scatter.9.cloned.1.call-start = ((), (), s32[]{:S(2)}) async-start(), calls=%async_computation.11 | async-start | bytes 4325376 | tf_op jit(solution)/shard_map/reduce_scatter | solution.py:72
  237.8 22.2 %copy-start.15 = (u32[128]{0:T(128)S(1)}, u32[128]{0:T(128)}, u32[]{:S(2)}) copy-start(u32[128]{0:T(128)} %constant.59) | copy-start | bytes 1540
  237.8 26.4 %copy-start.9 = (f32[2,4,32,256]{3,2,0,1:T(8,128)S(1)}, f32[2,4,32,256]{3,2,0,1:T(8,128)}, u32[]{:S(2)}) copy-start(f32[2,4,32,256]{3,2,0,1:T(8,128)} %all_to_all.15) | copy-start | bytes 786436
  255.9 8.3 all-to-all-start.1
  260.0 195.0 %all-gather.10.cloned.1.call-start = ((), (), s32[]{:S(2)}) async-start(), calls=%async_computation.9 | async-start | bytes 4325376 | tf_op jit(solution)/shard_map/all_gather | solution.py:79
  401.8 124.7 %all-gather.12.cloned.1.call-start = ((), (), s32[]{:S(2)}) async-start(), calls=%async_computation.12 | async-start | bytes 4325376 | tf_op jit(solution)/shard_map/all_gather | solution.py:79
  406.6 179.6 %reduce-scatter.7.cloned.1.call-start = ((), (), s32[]{:S(2)}) async-start(), calls=%async_computation.10 | async-start | bytes 4325376 | tf_op jit(solution)/shard_map/reduce_scatter | solution.py:87
  467.0 3.2 copy-start.2
  485.7 185.7 %reduce-scatter.11.cloned.1.call-start = ((), (), s32[]{:S(2)}) async-start(), calls=%async_computation.13 | async-start | bytes 4325376 | tf_op jit(solution)/shard_map/reduce_scatter | solution.py:87
  538.7 3.2 copy-start.3
  557.3 10.3 %copy-start.4 = (f32[4096,512]{0,1:T(8,128)S(1)}, f32[4096,512]{0,1:T(8,128)}, u32[]{:S(2)}) copy-start(f32[4096,512]{0,1:T(8,128)} %copy-done.3) | copy-start | bytes 25165828
  557.3 10.3 %copy-start.6 = (f32[1,128,32,256]{3,2,0,1:T(8,128)S(1)}, f32[1,128,32,256]{3,2,0,1:T(8,128)}, u32[]{:S(2)}) copy-start(f32[1,128,32,256]{3,2,0,1:T(8,128)} %copy-done.5) | copy-start | bytes 12582916
  557.3 17.0 %slice-start = ((s8[8388608]{0:T(1024)(128)(4,1)}), s8[4194304]{0:T(1024)(128)(4,1)S(1)}, s32[]{:S(2)}) async-start(s8[8388608]{0:T(1024)(128)(4,1)} %bitcast.73), calls=%async_computation.15 | async-start | bytes 8388608
  567.6 6.7 slice-start.1
  567.6 6.7 copy-start.14
  574.3 11.8 %copy-start.10 = (f32[128,256]{1,0:T(8,128)S(1)}, f32[128,256]{1,0:T(8,128)}, u32[]{:S(2)}) copy-start(f32[128,256]{1,0:T(8,128)} %get-tuple-element.10) | copy-start | bytes 393220
  574.4 97.1 %copy-start.11 = (f32[128,256]{1,0:T(8,128)S(1)}, f32[128,256]{1,0:T(8,128)}, u32[]{:S(2)}) copy-start(f32[128,256]{1,0:T(8,128)} %get-tuple-element.12) | copy-start | bytes 393220
  673.1 15.1 %all-to-all-start.2 = ((f32[2,4,32,256]{3,2,0,1:T(8,128)}), f32[2,4,32,256]{3,2,0,1:T(8,128)S(1)}, u32[]{:S(2)}, u32[]{:S(2)}) async-start(f32[2,4,32,256]{3,2,0,1:T(8,128)} %pad_maximum_fusion.1), calls=%async_computation.6 | async-start | bytes 524288 | tf_op jit(solution)/shard_map/all_to_all | solution.py:94
  677.2 11.3 %copy-start.13 = (s32[128]{0:T(128)S(1)}, s32[128]{0:T(128)}, u32[]{:S(2)}) copy-start(s32[128]{0:T(128)} %param.5) | copy-start | bytes 1540
  677.2 153.9 %all-reduce.6.cloned.1.call-start = ((), (), s32[]{:S(2)}) async-start(), calls=%async_computation.14 | async-start | bytes 131072 | tf_op jit(solution)/shard_map/psum | solution.py:96
  677.2 155.4 %copy-start.1 = (f32[64,256]{1,0:T(8,128)S(1)}, f32[64,256]{1,0:T(8,128)}, u32[]{:S(2)}) copy-start(f32[64,256]{1,0:T(8,128)} %param.6) | copy-start | bytes 196612
  688.5 144.1 %copy-start.12 = (f32[128,256]{1,0:T(8,128)}, f32[128,256]{1,0:T(8,128)S(1)}, u32[]{:S(2)}) copy-start(f32[128,256]{1,0:T(8,128)S(1)} %fusion.46) | copy-start | bytes 393220
Sparse Core Ops, SparseCore 0:
  22.0 53.9 all-gather.7
  237.5 82.1 reduce-scatter.4
  323.3 81.4 reduce-scatter.8
  407.6 47.4 all-gather.9
  457.7 45.2 all-gather.11
  506.5 79.5 reduce-scatter.6
  589.8 81.6 reduce-scatter.10
  689.6 141.4 all-reduce.5
where the time goes:
time: 847 us; the launch traced here: 840 us
  blocking collectives  342 us (40%)
  waiting for transfers between devices  294 us (35%)
  matrix products  146 us (17%)
  other arithmetic  18.8 us (2%)
  between operations  15.4 us (2%)
  local copies, waits for them, and re-layouts  14.2 us (2%)
  starting transfers between devices  8.93 us (1%)
    dot_general x16, matrix products, contract(): lax.dot_general(former, latter, (((former_dim,), (latter_dim,)), ((), ())...  146 us
    psum x1, waiting for transfers between devices, per_device(): lax.psum(-contract(onehot, item_grad, 0, 0), ('group', 'shard'))  141 us
    unnamed x1, blocking collectives  126 us
    pmax x1, blocking collectives, per_device(): peak_score = lax.pmax(jnp.max(scores, axis=1), 'shard')  121 us
    reduce_scatter x2, waiting for transfers between devices, per_device(): lax.psum_scatter(pushed, 'shard', scatter_dimension=0, tiled=True)  88.1 us
    all_gather x1, waiting for transfers between devices, per_device(): lax.all_gather(arrived, 'shard', axis=1, tiled=True)  54.1 us
    all_gather x2, blocking collectives, per_device(): lax.all_gather(denominator_own, 'shard', axis=0, tiled=True)  43.4 us
    all_gather x2, blocking collectives, per_device(): lax.all_gather(own_inner, 'shard', axis=0, tiled=True)  40.5 us
  transfers between devices with their start and end apart: 10, of which 7 were waited for; matrix products, arithmetic and copies ran while one was open for 15% of the time, Pallas kernels for 0%

commit v1 on v0

v1 whole, which is shorter than its diff:
```python
import functools

import jax
import jax.numpy as jnp
from jax import lax
from jax.experimental import pallas as pl
from jax.experimental.pallas import tpu as pltpu
from jax.sharding import Mesh, PartitionSpec as P


sharpness = 2.5
LOG2E = 1.4426950408889634
F32 = jnp.float32
BF16 = jnp.bfloat16
AXES = ("z", "x", "y", "c")
SLOTS = 32
BLOCK = 40
HOLD = 136
CHUNK = 512


def dot_nn(a, b):
    return lax.dot_general(a, b, (((1,), (0,)), ((), ())), preferred_element_type=F32)


def dot_nt(a, b):
    return lax.dot_general(a, b, (((1,), (1,)), ((), ())), preferred_element_type=F32)


def split2(value):
    high = value.astype(BF16)
    return high, (value - high.astype(F32)).astype(BF16)


def split3(value):
    high = value.astype(BF16)
    rest = value - high.astype(F32)
    middle = rest.astype(BF16)
    return high, middle, (rest - middle.astype(F32)).astype(BF16)


def select_rows(onehot, value):
    chosen = onehot.astype(BF16)
    high, middle, low = split3(value)
    return (dot_nn(chosen, low) + dot_nn(chosen, middle)) + dot_nn(chosen, high)


def iota(shape, dim):
    return lax.broadcasted_iota(jnp.int32, shape, dim)


def targets(code_row, items):
    group_row = code_row // 8
    wide = jnp.broadcast_to(group_row.astype(F32), (items, items))
    same = (jnp.transpose(wide) == wide) & (iota((items, items), 0) < iota((items, items), 1))
    place_row = jnp.sum(same.astype(F32), axis=0, keepdims=True).astype(jnp.int32)
    return group_row, place_row


def route_kernel(z_ref, codes_ref, vectors_ref, coarse_ref, out_ref):
    items, coarse_total = vectors_ref.shape[0], coarse_ref.shape[0]
    code_row = codes_ref[...]
    group_row, place_row = targets(code_row, items)
    code_column = jnp.transpose(jnp.broadcast_to(code_row.astype(F32), (items, items))).astype(jnp.int32)
    onehot = (code_column[:, 0:coarse_total] == iota((items, coarse_total), 1)).astype(F32)
    residual = vectors_ref[...] - select_rows(onehot, coarse_ref[...])
    total = out_ref.shape[0]
    target_row = group_row * BLOCK + place_row
    placing = (iota((total, items), 0) == target_row).astype(F32)
    out_ref[...] = select_rows(placing, residual)
    groups = total // BLOCK
    inner = (code_row - group_row * 8 + 1).astype(F32)
    marks = jnp.where(iota((groups, items), 0) == group_row, inner, 0.0).astype(BF16)
    spots = (iota((items, items), 0) == place_row + SLOTS * z_ref[0]).astype(F32).astype(BF16)
    info = dot_nt(marks, spots)
    for g in range(groups):
        out_ref[g * BLOCK + SLOTS : g * BLOCK + SLOTS + 1, 0:items] = info[g : g + 1, :]


def fetch(blocks, g, book_ref, sems, b):
    source = blocks[b] if len(blocks[b].shape) == 2 else blocks[b].at[g]
    return pltpu.make_async_copy(source, book_ref.at[b], sems.at[b])


def landed(ref, sems, b):
    pltpu.make_async_copy(ref.at[b], ref.at[b], sems.at[b]).wait()


def forward_kernel(g, rows_ref, *refs):
    blocks = refs[:8]
    high_ref, low_ref, part_ref = refs[8:11]
    (score_ref, triple_ref, book_ref, keep_high, keep_low, wide_high, wide_low) = refs[11:18]
    peak_ref, total_ref, quant_ref, sems, high_sems, low_sems = refs[18:]
    count = score_ref.shape[1]
    for b in range(8):
        fetch(blocks, g, book_ref, sems, b).start()
    rows = rows_ref[:, :, g].reshape(count, -1) * (sharpness * LOG2E)
    high, low = split2(rows)
    triple_ref[...] = jnp.concatenate([high, high, low], axis=1)
    peak_ref[...] = jnp.full(peak_ref.shape, -jnp.inf, F32)
    total_ref[...] = jnp.zeros(total_ref.shape, F32)
    quant_ref[...] = jnp.zeros(quant_ref.shape, F32)

    @pl.loop(0, 8)
    def _(b):
        landed(book_ref, sems, b)
        ch, cl = split2(book_ref[b])
        keep_high[b] = ch
        keep_low[b] = cl
        right = jnp.concatenate([ch, cl, ch], axis=1)
        peak = peak_ref[...]
        for half in range(2):
            s = dot_nt(triple_ref[...], right[half * 256 : (half + 1) * 256])
            score_ref[b, :, half * 256 : (half + 1) * 256] = s
            peak = jnp.maximum(peak, jnp.maximum(s[:, 0:128], s[:, 128:256]))
        peak_ref[...] = peak

    peak_ref[...] = jnp.broadcast_to(jnp.max(peak_ref[...], axis=1, keepdims=True), peak_ref.shape)

    @pl.loop(0, 8)
    def _(b):
        peak = peak_ref[...]
        total = total_ref[...]
        left, right = [], []
        for half in range(2):
            at = slice(half * 256, (half + 1) * 256)
            w = jnp.exp2(score_ref[b, :, at] - jnp.concatenate([peak, peak], axis=1))
            total = total + (w[:, 0:128] + w[:, 128:256])
            wh, wl = split2(w)
            wide_high[b, :, at] = wh
            wide_low[b, :, at] = wl
            left += [wh, wl, wh]
            ch = keep_high[b, at, :]
            right += [ch, ch, keep_low[b, at, :]]
        total_ref[...] = total
        quant_ref[...] += dot_nn(jnp.concatenate(left, axis=1), jnp.concatenate(right, axis=0))
        pltpu.make_async_copy(wide_high.at[b], high_ref.at[b], high_sems.at[b]).start()
        pltpu.make_async_copy(wide_low.at[b], low_ref.at[b], low_sems.at[b]).start()

    held = count // 4
    lane = iota((held, 128), 1)
    total = jnp.sum(total_ref[...], axis=1, keepdims=True)
    mixed = jnp.zeros((held, 128), F32)
    for y in range(4):
        mine = slice(y * held, (y + 1) * held)
        part_ref[y, 0:held, :] = quant_ref[mine]
        mixed = jnp.where(lane == 8 * y, peak_ref[mine], mixed)
        mixed = jnp.where(lane == 8 * y + 1, total[mine], mixed)
    mixed = jnp.transpose(mixed)
    for y in range(4):
        part_ref[y, held:HOLD, 0:held] = mixed[8 * y : 8 * y + 8]
        part_ref[y, held:HOLD, held:] = jnp.zeros((8, part_ref.shape[2] - held), F32)
    for b in range(8):
        pltpu.make_async_copy(wide_high.at[b], high_ref.at[b], high_sems.at[b]).wait()
        pltpu.make_async_copy(wide_low.at[b], low_ref.at[b], low_sems.at[b]).wait()


def columns(tiles):
    size = tiles[0].shape[1]
    stacked = jnp.concatenate(tiles, axis=0)
    rest = size - stacked.shape[0]
    if rest:
        stacked = jnp.concatenate([stacked, jnp.zeros((rest, size), F32)], axis=0)
    return jnp.transpose(stacked)


def merge_kernel(part_ref, info_ref, out_ref):
    held = 128
    code_row = functools.reduce(jnp.add, [info_ref[z, 0, SLOTS : SLOTS + 1, 0:held] for z in range(4)])
    turned = columns([part_ref[y, held:HOLD, 0:held] for y in range(4)] + [jnp.broadcast_to(code_row, (8, held))])
    peaks = [turned[:, 8 * y : 8 * y + 1] for y in range(4)]
    totals = [turned[:, 8 * y + 1 : 8 * y + 2] for y in range(4)]
    peak = functools.reduce(jnp.maximum, peaks)
    scales = [jnp.exp2(p - peak) for p in peaks]
    total = functools.reduce(jnp.add, [t * s for t, s in zip(totals, scales)])
    live = turned[:, 32:33] > 0.5
    quant = functools.reduce(jnp.add, [part_ref[y, 0:held, :] * scales[y] for y in range(4)])
    quant = jnp.where(live, quant / total, 0.0)
    lane = iota((held, held), 1)
    mixed = jnp.where(lane == 0, peak, jnp.where(lane == 1, total, turned[:, 32:33]))
    info = jnp.transpose(mixed)[0:8]
    for y in range(4):
        out_ref[y, 0:held, :] = quant
        out_ref[y, held:HOLD, 0:held] = info
        out_ref[y, held:HOLD, held:] = jnp.zeros((8, out_ref.shape[2] - held), F32)


def backward_kernel(g, first, number, resumed, final, joined, y_ref, rows_ref, part_ref, merged_ref, high_ref, low_ref, *refs):
    blocks = refs[:8]
    refs = refs[8:]
    if resumed:
        before_ref, refs = refs[0], refs[1:]
    if joined:
        (push0_ref, coarse0_ref), refs = refs[:2], refs[2:]
    (own_ref, other_ref), refs = refs[:2], refs[2:]
    if joined:
        pushed_ref, refs = refs[0], refs[1:]
    elif final:
        (pushed_ref, coarse_ref), refs = refs[:2], refs[2:]
    else:
        (sofar_ref,), refs = refs[:1], refs[1:]
    triple_ref, left_ref, inner_ref, error_ref, total_ref, book_ref, wide_high, wide_low, wide_grads = refs[:9]
    sems, high_sems, low_sems, grads_sems = refs[9:]
    count, width = error_ref.shape
    held = count // 4

    def loads(b):
        return (
            fetch(blocks, g, book_ref, sems, b),
            pltpu.make_async_copy(high_ref.at[b], wide_high.at[b], high_sems.at[b]),
            pltpu.make_async_copy(low_ref.at[b], wide_low.at[b], low_sems.at[b]),
        )

    for b in range(first, first + number):
        for load in loads(b):
            load.start()
    turned = columns([ref[y, held:HOLD, 0:held] for y in range(4) for ref in (part_ref, merged_ref)])
    for y in range(4):
        mine = slice(y * held, (y + 1) * held)
        at = 16 * y
        factor = jnp.exp2(turned[:, at : at + 1] - turned[:, at + 8 : at + 9]) / turned[:, at + 9 : at + 10]
        rows = rows_ref[y, :, g].reshape(held, width)
        quant = merged_ref[y, 0:held, :]
        error = jnp.where(turned[:, at + 10 : at + 11] > 0.5, quant - rows, 0.0)
        inner = jnp.sum(error * quant, axis=1, keepdims=True) * factor
        scaled = error * factor
        error_ref[mine] = error
        inner_ref[mine] = jnp.broadcast_to(inner, (held, 128))
        high, low = split2(scaled)
        triple_ref[mine] = jnp.concatenate([high, high, low], axis=1)
        for k, value in enumerate((scaled, rows * sharpness)):
            high, low = split2(jnp.transpose(value))
            for part, piece in enumerate((high, low, high)):
                left_ref[:, (3 * k + part) * count + y * held : (3 * k + part) * count + (y + 1) * held] = piece
    if resumed:
        total_ref[...] = before_ref[...]
    else:
        total_ref[...] = jnp.zeros(total_ref.shape, F32)

    @pl.loop(first, first + number)
    def _(b):
        pair = (b - first) // 2
        landed(book_ref, sems, b)
        landed(wide_high, high_sems, b)
        landed(wide_low, low_sems, b)
        ch, cl = split2(book_ref[b])
        right = jnp.concatenate([ch, cl, ch], axis=1)
        inner = inner_ref[...]
        highs, lows = [], []
        for half in range(2):
            align = dot_nt(triple_ref[...], right[half * 256 : (half + 1) * 256])
            for t in range(2):
                at = slice(half * 256 + t * 128, half * 256 + t * 128 + 128)
                w = wide_high[b, :, at].astype(F32) + wide_low[b, :, at].astype(F32)
                sh, sl = split2(w * (align[:, t * 128 : (t + 1) * 128] - inner))
                highs.append(sh)
                lows.append(sl)
        sh = jnp.concatenate(highs, axis=1)
        sl = jnp.concatenate(lows, axis=1)
        wh, wl = wide_high[b], wide_low[b]
        wide_grads[b] = dot_nn(left_ref[...], jnp.concatenate([wh, wh, wl, sh, sh, sl], axis=0))

        @pl.when(b % 2 == 0)
        def _():
            pltpu.make_async_copy(wide_grads.at[b], own_ref.at[pair], grads_sems.at[b]).start()

        @pl.when(b % 2 == 1)
        def _():
            pltpu.make_async_copy(wide_grads.at[b], other_ref.at[pair], grads_sems.at[b]).start()

        total_ref[...] += dot_nn(jnp.concatenate([sh, sl, sh], axis=1), jnp.concatenate([ch, ch, cl], axis=0))

    if final:
        rest = held if joined else 0
        code_row = jnp.concatenate([merged_ref[y, held + 2 : held + 3, 0:held] for y in range(4)], axis=1)
        onehot = (iota((8, count), 0) + 1 == code_row.astype(jnp.int32)).astype(F32)
        coarse = jnp.zeros((8, width), F32)
        for y in range(4):
            mine = slice(y * held, (y + 1) * held)
            pushed = total_ref[mine] * sharpness - jnp.where(y_ref[0] == y, error_ref[mine], 0.0)
            pushed_ref[y, rest : rest + held] = pushed
            coarse = coarse - select_rows(onehot[:, mine], pushed)
        if joined:
            for y in range(4):
                pushed_ref[y, 0:held] = push0_ref[y]
                pushed_ref[y, 2 * held : 2 * held + 8] = coarse0_ref[...]
                pushed_ref[y, 2 * held + 8 : 2 * held + 16] = coarse
        else:
            coarse_ref[...] = coarse
    else:
        sofar_ref[...] = total_ref[...]
    for b in range(first, first + number):
        out = own_ref if b % 2 == 0 else other_ref
        pltpu.make_async_copy(wide_grads.at[b], out.at[(b - first) // 2], grads_sems.at[b]).wait()


def turn_kernel(own_ref, other_ref, right_ref, left_ref, far_ref, *refs):
    near = (own_ref[0] + other_ref[0]) + (right_ref[...] + left_ref[...])
    refs[-1][0] = jnp.transpose(near + far_ref[...])


def home_kernel(codes_ref, slots_ref, out_ref):
    items, width = out_ref.shape
    group_row, place_row = targets(codes_ref[...], items)
    total = slots_ref.shape[0] * slots_ref.shape[1]
    target = (group_row // 2) * slots_ref.shape[1] + (group_row % 2) * SLOTS + place_row
    target = jnp.transpose(jnp.broadcast_to(target.astype(F32), (items, items)))[:, 0:1].astype(jnp.int32)
    onehot = (target == iota((items, total), 1)).astype(F32)
    out_ref[...] = select_rows(onehot, slots_ref[...].reshape(total, width))


def params(mebibytes=8):
    return pltpu.CompilerParams(vmem_limit_bytes=mebibytes << 20)


def whole(shape, dtype=F32):
    return jax.ShapeDtypeStruct(shape, dtype)


SMEM = pl.BlockSpec(memory_space=pltpu.SMEM)
VMEM = pl.BlockSpec(memory_space=pltpu.VMEM)
ANY = pl.BlockSpec(memory_space=pl.ANY)


def cost(flops, moved, exps=0):
    return pl.CostEstimate(flops=flops, bytes_accessed=moved, transcendentals=exps)


def dmas():
    return pltpu.SemaphoreType.DMA((8,))


def forward(g, rows, blocks):
    width = rows.shape[-1]
    count = 512
    return pl.pallas_call(
        functools.partial(forward_kernel, g),
        in_specs=[VMEM] + [ANY] * 8,
        out_specs=[ANY, ANY, VMEM],
        out_shape=[
            whole((8, count, CHUNK), BF16),
            whole((8, count, CHUNK), BF16),
            whole((4, HOLD, width)),
        ],
        scratch_shapes=[
            pltpu.VMEM((8, count, CHUNK), F32),
            pltpu.VMEM((count, 3 * width), BF16),
            pltpu.VMEM((8, CHUNK, width), F32),
            pltpu.VMEM((8, CHUNK, width), BF16),
            pltpu.VMEM((8, CHUNK, width), BF16),
            pltpu.VMEM((8, count, CHUNK), BF16),
            pltpu.VMEM((8, count, CHUNK), BF16),
            pltpu.VMEM((count, 128), F32),
            pltpu.VMEM((count, 128), F32),
            pltpu.VMEM((count, width), F32),
            dmas(),
            dmas(),
            dmas(),
        ],
        compiler_params=params(60),
        cost_estimate=cost(12 * count * 8 * CHUNK * width, 12 * count * 8 * CHUNK, count * 8 * CHUNK),
    )(rows, *blocks)


def backward(g, first, number, y, rows, part, merged, weights, blocks, before, final, joined=()):
    width = rows.shape[-1]
    count = 512
    resumed = before is not None
    out_shape = [whole((number // 2, width, CHUNK))] * 2
    if joined:
        out_shape += [whole((4, count // 2 + 16, width))]
    elif final:
        out_shape += [whole((4, count // 4, width)), whole((8, width))]
    else:
        out_shape += [whole((count, width))]
    return pl.pallas_call(
        functools.partial(backward_kernel, g, first, number, resumed, final, bool(joined)),
        in_specs=[SMEM, VMEM, VMEM, VMEM] + [ANY] * 10 + [VMEM] * (resumed + len(joined)),
        out_specs=[ANY, ANY] + [VMEM] * (len(out_shape) - 2),
        out_shape=out_shape,
        scratch_shapes=[
            pltpu.VMEM((count, 3 * width), BF16),
            pltpu.VMEM((width, 6 * count), BF16),
            pltpu.VMEM((count, 128), F32),
            pltpu.VMEM((count, width), F32),
            pltpu.VMEM((count, width), F32),
            pltpu.VMEM((8, CHUNK, width), F32),
            pltpu.VMEM((8, count, CHUNK), BF16),
            pltpu.VMEM((8, count, CHUNK), BF16),
            pltpu.VMEM((8, width, CHUNK), F32),
            dmas(),
            dmas(),
            dmas(),
            dmas(),
        ],
        compiler_params=params(60),
        cost_estimate=cost(24 * count * number * CHUNK * width, 8 * count * number * CHUNK),
    )(y, rows, part, merged, *weights, *blocks, *((before,) if resumed else ()), *joined)


def after(value, *others):
    return lax.optimization_barrier((value,) + others)[0]


def step(vectors, item_codes, coarse_book, fine_books):
    items, width = vectors.shape
    shift = lambda a, axis, by: lax.ppermute(a, axis, [(i, (i + by) % 4) for i in range(4)])
    swap = lambda a: lax.ppermute(a, "c", [(0, 1), (1, 0)])
    code_row = item_codes.reshape(1, items)
    z = lax.axis_index("z").astype(jnp.int32).reshape(1)
    y = lax.axis_index("y").astype(jnp.int32).reshape(1)

    def travel(book):
        return [shift(book, "x", by) for by in (1, -1, 2)]

    own = [fine_books[0], fine_books[1]]
    near = [travel(own[0])]
    outgoing = pl.pallas_call(
        route_kernel,
        in_specs=[SMEM, VMEM, VMEM, VMEM],
        out_specs=VMEM,
        out_shape=whole((8 * BLOCK, width)),
        compiler_params=params(),
        name="route",
    )(z, code_row, vectors, coarse_book)
    arrived = lax.all_to_all(outgoing.reshape(4, 2 * BLOCK, width), "z", 0, 0, tiled=True)
    near.append(travel(after(own[1], arrived)))
    arrived = arrived.reshape(4, 2, BLOCK, width)
    spread = jnp.broadcast_to(arrived[None, :, :, :SLOTS], (4, 4, 2, SLOTS, width))
    rows = lax.all_to_all(spread, "y", 0, 0, tiled=True)

    books, weights, parts = [], [], []
    for g in range(2):
        left, right, far = near[g]
        if g:
            left, right, far, own[g], _ = lax.optimization_barrier((left, right, far, own[g], parts[0]))
        blocks = []
        for book in (far, left, right, own[g]):
            blocks += [book, swap(book)]
        *weight, part = forward(g, rows, blocks)
        books.append(blocks)
        weights.append(weight)
        parts.append(part)

    def exchange(g, part):
        got = lax.all_to_all(part, "y", 0, 0, tiled=True)
        out = pl.pallas_call(
            merge_kernel,
            grid=(1,),
            in_specs=[
                pl.BlockSpec((4, HOLD, width), lambda i: (0, 0, 0)),
                pl.BlockSpec((4, 1, BLOCK, width), lambda i: (0, g, 0, 0)),
            ],
            out_specs=pl.BlockSpec((4, HOLD, width), lambda i: (0, 0, 0)),
            out_shape=whole((4, HOLD, width)),
            compiler_params=params(),
        )(got, arrived)
        return lax.all_to_all(out, "y", 0, 0, tiled=True)

    merged = [exchange(0, parts[0])]
    merged.append(exchange(1, after(parts[1], merged[0])))

    def return_books(g, calls, before):
        pieces = []
        for when, (own, other) in enumerate(calls):
            got = swap(other)
            pieces += [(own, got, i, when) for i in range(own.shape[0])]
        got = []
        for (own, other, i, when), by in zip(pieces, (2, -1, 1)):
            total = own[i] + other[i]
            got.append(shift(total, "x", by))
        own, other, i, _ = pieces[3]
        pair = pl.BlockSpec((1, width, CHUNK), lambda k: (i, 0, 0))
        flat = pl.BlockSpec((width, CHUNK), lambda k: (0, 0))
        return pl.pallas_call(
            turn_kernel,
            grid=(1,),
            in_specs=[pair, pair, flat, flat, flat] + [ANY] * len(before),
            out_specs=pl.BlockSpec((1, CHUNK, width), lambda k: (g, 0, 0)),
            out_shape=whole((2, CHUNK, width)),
            input_output_aliases={5: 0} if before else {},
            compiler_params=params(),
        )(own, other, *got, *before)

    def gradients(g, counts, joined, before):
        common = (y, rows, parts[g], merged[g], weights[g], books[g])
        calls, first, sofar = [], 0, None
        for number in counts:
            final = first + number == 8
            own, other, *rest = backward(g, first, number, *common, sofar, final, joined if final else ())
            calls.append((own, other))
            first, sofar = first + number, rest[0]
        return return_books(g, calls, before), rest

    fine, joined = gradients(0, (4, 4), (), ())
    fine, (push,) = gradients(1, (4, 2, 2), tuple(joined), (fine,))

    held = items
    push = lax.all_to_all(push, "y", 0, 0, tiled=True)
    push = jnp.sum(push, axis=0)
    coarse = push[2 * held :]
    push = push[: 2 * held].reshape(2, 4, SLOTS, width).transpose(1, 0, 2, 3).reshape(4, 2 * SLOTS, width)
    push = jnp.concatenate([push, jnp.broadcast_to(coarse[None], (4,) + coarse.shape)], axis=1)
    home = lax.all_to_all(push, "z", 0, 0, tiled=True)
    coarse = home[:, 2 * SLOTS :].reshape(-1, width)
    coarse = coarse + swap(coarse)
    others = [shift(coarse, "x", by) for by in (1, 2, 3)]
    coarse = (coarse + others[1]) + (others[0] + others[2])
    item_grad = pl.pallas_call(
        home_kernel,
        in_specs=[VMEM, VMEM],
        out_specs=VMEM,
        out_shape=whole((items, width)),
        compiler_params=params(),
        name="home",
    )(code_row, home)
    return item_grad, fine, coarse


def solution(mesh):
    grid = Mesh(mesh.devices.reshape(4, 4, 4, 2), AXES)
    plane = ("x", "y", "c")
    return jax.shard_map(
        step,
        mesh=grid,
        in_specs=(P(AXES, None), P(AXES), P(), P("z", plane, None)),
        out_specs=(P(AXES, None), P("z", plane, None), P()),
        check_vma=False,
    )
```

time: 847 us -> 239 us (0.28)
  blocking collectives: 342 us -> 11.1 us
  waiting for transfers between devices: 294 us -> 56.5 us
  matrix products: 146 us -> 0 us
  Pallas kernels: 0 us -> 90.5 us
  starting transfers between devices: 8.93 us -> 59.3 us
  between operations: 15.4 us -> 0.98 us
  other arithmetic: 18.8 us -> 10.2 us
    dot_general x16 -> x0, matrix products: 146 us -> none  [contract(): lax.dot_general(former, latter, (((former_dim,), (latter_dim,)), ((), ())...]
    psum x1 -> x0, waiting for transfers between devices: 141 us -> none  [per_device(): lax.psum(-contract(onehot, item_grad, 0, 0), ('group', 'shard'))]
    unnamed x1 -> x0, blocking collectives: 126 us -> none
    pmax x1 -> x0, blocking collectives: 121 us -> none  [per_device(): peak_score = lax.pmax(jnp.max(scores, axis=1), 'shard')]
    reduce_scatter x4 -> x0, waiting for transfers between devices: 90.9 us -> none  [the longest x2 88.1 us: per_device(): lax.psum_scatter(pushed, 'shard', scatter_dimension=0, tiled=True)]
    pallas_call x0 -> x13, Pallas kernels: none -> 90.5 us  [the longest x5 54.7 us: backward(): pl.pallas_call(functools.partial(backward_kernel, g, first, number, resum...]
    all_gather x4 -> x0, blocking collectives: 83.9 us -> none  [the longest x2 43.4 us: per_device(): lax.all_gather(denominator_own, 'shard', axis=0, tiled=True)]
    all_gather x3 -> x0, waiting for transfers between devices: 59.1 us -> none  [the longest x1 54.1 us: per_device(): lax.all_gather(arrived, 'shard', axis=1, tiled=True)]
  transfers between devices with their start and end apart: 10 -> 36, of which waited for: 7 -> 9; matrix products, arithmetic and copies ran while one was open for 15% -> 5% of each run, Pallas kernels for 0% -> 37%
where the time goes in v1:
time: 239 us; the launch traced here: 236 us
  Pallas kernels  90.5 us (38%)
  starting transfers between devices  59.3 us (25%)
  waiting for transfers between devices  56.5 us (24%)
  blocking collectives  11.1 us (5%)
  other arithmetic  10.2 us (4%)
  local copies, waits for them, and re-layouts  7.44 us (3%)
    pallas_call x5, Pallas kernels, backward(): pl.pallas_call(functools.partial(backward_kernel, g, first, number, resum...  54.7 us
    ppermute x15, waiting for transfers between devices, step(): lax.ppermute(a, axis, [(i, (i + by) % 4) for i in range(4)])  32 us
    pallas_call x2, Pallas kernels, forward(): pl.pallas_call(functools.partial(forward_kernel, g), in_specs=[VMEM] + [A...  28 us
    ppermute x15, starting transfers between devices, step(): lax.ppermute(a, axis, [(i, (i + by) % 4) for i in range(4)])  15.5 us
    ppermute x14, starting transfers between devices, step(): swap = lambda a: lax.ppermute(a, 'c', [(0, 1), (1, 0)])  14 us
    all_to_all x1, blocking collectives, step(): lax.all_to_all(outgoing.reshape(4, 2 * BLOCK, width), 'z', 0, 0, tiled=True)  11.1 us
    all_to_all x2, waiting for transfers between devices, exchange(): got = lax.all_to_all(part, 'y', 0, 0, tiled=True)  9.16 us
    all_to_all x2, starting transfers between devices, exchange(): got = lax.all_to_all(part, 'y', 0, 0, tiled=True)  8.38 us
  transfers between devices with their start and end apart: 36, of which 9 were waited for; matrix products, arithmetic and copies ran while one was open for 5% of the time, Pallas kernels for 37%

profile of v1, /device:TPU:1, one launch (start us, length us, event | category | flops | bytes accessed | tf_op | source)
XLA Modules:
  0.0 236.0 jit_solution(14939160801318979314)
XLA Ops:
  1.9 3.4 %collective-permute-start.7 = (f32[512,256]{1,0:T(8,128)S(1)}, f32[512,256]{1,0:T(8,128)S(1)}, u32[]{:S(2)}, u32[]{:S(2)}) collective-permute-start(f32[512,256]{1,0:T(8,128)S(1)} %get-tuple-element.63.refs_6_), channel_id=1, source_target_pairs={{0,24},{8,0},{16,8},{24,16},{1,25},{9,1},{17,9},{25,17},{2,26},{10... | collective-permute-start | bytes 1572872 | tf_op jit(solution)/shard_map/ppermute | solution.py:407
  10.0 11.1 %all_to_all.40 = f32[4,80,256]{2,1,0:T(8,128)S(1)} all-to-all(f32[4,80,256]{2,1,0:T(8,128)S(1)} %bitcast.30), channel_id=1, replica_groups=mesh['z'=4,'x'=4,'y'=4,'c'=2] {'z'}, dimensions={0} | all-to-all | bytes 655360 | tf_op jit(solution)/shard_map/all_to_all | solution.py:426
  22.2 4.2 %all-to-all-start.1 = ((f32[4,4,2,32,256]{4,3,2,1,0:T(8,128)}), f32[4,4,2,32,256]{4,3,2,1,0:T(8,128)S(1)}, u32[]{:S(2)}, u32[]{:S(2)}) async-start(f32[4,4,2,32,256]{4,3,2,1,0:T(8,128)} %broadcast_in_dim.4), calls=%async_computation.1 | async-start | bytes 2097152 | tf_op jit(solution)/shard_map/all_to_all | solution.py:430
  26.4 2.8 %collective-permute-start.9 = (f32[512,256]{1,0:T(8,128)S(1)}, f32[512,256]{1,0:T(8,128)S(1)}, u32[]{:S(2)}, u32[]{:S(2)}) collective-permute-start(f32[512,256]{1,0:T(8,128)S(1)} %get-tuple-element.63.refs_6_), channel_id=1, source_target_pairs={{0,1},{1,0},{2,3},{3,2},{4,5},{5,4},{6,7},{7,6},{8,9},{9,8},{10,11... | collective-permute-start | bytes 1572872 | tf_op jit(solution)/shard_map/ppermute | solution.py:408
  29.4 2.8 %collective-permute-start.6 = (f32[512,256]{1,0:T(8,128)}, f32[512,256]{1,0:T(8,128)}, u32[]{:S(2)}, u32[]{:S(2)}) collective-permute-start(f32[512,256]{1,0:T(8,128)} %collective-permute-done.5.refs_2_), channel_id=1, source_target_pairs={{0,1},{1,0},{2,3},{3,2},{4,5},{5,4},{6,7},{7,6},{8,9},{9,8},{10,11... | collective-permute-start | bytes 1572872 | tf_op jit(solution)/shard_map/ppermute | solution.py:408
  34.8 4.0 %all-to-all-done.1.rows_ref = f32[4,4,2,32,256]{4,3,2,1,0:T(8,128)S(1)} async-done(((f32[4,4,2,32,256]{4,3,2,1,0:T(8,128)}), f32[4,4,2,32,256]{4,3,2,1,0:T(8,128)S(1)}, u32[]{:S(2)}, u32[]{:S(2)}) %all-to-all-start.1) | async-done | bytes 1048608 | tf_op jit(solution)/shard_map/all_to_all | solution.py:430
  39.8 14.0 %shard_map.67 = (bf16[8,512,512]{2,1,0:T(8,128)(2,1)}, bf16[8,512,512]{2,1,0:T(8,128)(2,1)}, f32[4,136,256]{2,1,0:T(8,128)}) custom-call(f32[4,4,2,32,256]{4,3,2,1,0:T(8,128)} %copy-done.6, f32[512,256]{1,0:T(8,128)} %collective-permute-done.3.refs_0_, f32[512,256]{1,0:T(8,128)} %collective-permute-done.4.refs_1_, ...), custom_call_target="tpu_custom_call" | custom-call | flops 6442450944 | bytes 25165824 | tf_op jit(solution)/shard_map/pallas_call | solution.py:336
  53.8 2.6 %collective-permute-done.1.refs_4_ = f32[512,256]{1,0:T(8,128)S(1)} collective-permute-done((f32[512,256]{1,0:T(8,128)S(1)}, f32[512,256]{1,0:T(8,128)S(1)}, u32[]{:S(2)}, u32[]{:S(2)}) %collective-permute-start.1) | collective-permute-done | bytes 524320 | tf_op jit(solution)/shard_map/ppermute | solution.py:407
  56.4 2.4 %collective-permute-done.refs_2_ = f32[512,256]{1,0:T(8,128)S(1)} collective-permute-done((f32[512,256]{1,0:T(8,128)S(1)}, f32[512,256]{1,0:T(8,128)S(1)}, u32[]{:S(2)}, u32[]{:S(2)}) %collective-permute-start) | collective-permute-done | bytes 524320 | tf_op jit(solution)/shard_map/ppermute | solution.py:407
  59.8 4.2 %all-to-all-start.2 = ((f32[4,136,256]{2,1,0:T(8,128)}), f32[4,136,256]{2,1,0:T(8,128)S(1)}, u32[]{:S(2)}, u32[]{:S(2)}) async-start(f32[4,136,256]{2,1,0:T(8,128)} %get-tuple-element.32.part_ref), calls=%async_computation.2 | async-start | bytes 1114112 | tf_op jit(solution)/shard_map/all_to_all | solution.py:446
  64.0 9.2 %all-to-all-done.2.part_ref = f32[4,136,256]{2,1,0:T(8,128)S(1)} async-done(((f32[4,136,256]{2,1,0:T(8,128)}), f32[4,136,256]{2,1,0:T(8,128)S(1)}, u32[]{:S(2)}, u32[]{:S(2)}) %all-to-all-start.2) | async-done | bytes 557088 | tf_op jit(solution)/shard_map/all_to_all | solution.py:446
  74.5 3.5 %all-to-all-start.3 = ((f32[4,136,256]{2,1,0:T(8,128)}), f32[4,136,256]{2,1,0:T(8,128)S(1)}, u32[]{:S(2)}, u32[]{:S(2)}) async-start(f32[4,136,256]{2,1,0:T(8,128)} %shard_map.69), calls=%async_computation.3 | async-start | bytes 1114112 | tf_op jit(solution)/shard_map/all_to_all | solution.py:458
  78.1 14.0 %shard_map.68 = (bf16[8,512,512]{2,1,0:T(8,128)(2,1)}, bf16[8,512,512]{2,1,0:T(8,128)(2,1)}, f32[4,136,256]{2,1,0:T(8,128)}) custom-call(f32[4,4,2,32,256]{4,3,2,1,0:T(8,128)} %copy-done.6, f32[512,256]{1,0:T(8,128)} %copy-done.9, f32[512,256]{1,0:T(8,128)} %collective-permute-done.10.refs_1_, f32[512,256]{1,0:T(8,128)} %copy-done.11, ...), custom_call_target="tpu_custom_call" | custom-call | flops 6442450944 | bytes 25165824 | tf_op jit(solution)/shard_map/pallas_call | solution.py:336
  92.1 4.2 %all-to-all-start.4 = ((f32[4,136,256]{2,1,0:T(8,128)}), f32[4,136,256]{2,1,0:T(8,128)S(1)}, u32[]{:S(2)}, u32[]{:S(2)}) async-start(f32[4,136,256]{2,1,0:T(8,128)} %get-tuple-element.38.part_ref), calls=%async_computation.4 | async-start | bytes 1114112 | tf_op jit(solution)/shard_map/all_to_all | solution.py:446
  96.3 12.3 %shard_map.73 = (f32[2,256,512]{2,1,0:T(8,128)}, f32[2,256,512]{2,1,0:T(8,128)}, f32[512,256]{1,0:T(8,128)}) custom-call(s32[1]{0:T(128)} %bitcast.1.y_ref, f32[4,4,2,32,256]{4,3,2,1,0:T(8,128)} %copy-done.6, f32[4,136,256]{2,1,0:T(8,128)} %get-tuple-element.32.part_ref, f32[4,136,256]{2,1,0:T(8,128)} %copy-done.12, ...), custom_call_target="tpu_custom_call" | custom-call | flops 6442450944 | bytes 8388608 | tf_op jit(solution)/shard_map/pallas_call | solution.py:376
  110.0 4.2 %all-to-all-start.5 = ((f32[4,136,256]{2,1,0:T(8,128)}), f32[4,136,256]{2,1,0:T(8,128)S(1)}, u32[]{:S(2)}, u32[]{:S(2)}) async-start(f32[4,136,256]{2,1,0:T(8,128)} %shard_map.70), calls=%async_computation.5 | async-start | bytes 1114112 | tf_op jit(solution)/shard_map/all_to_all | solution.py:458
  114.3 12.4 %shard_map.74 = (f32[2,256,512]{2,1,0:T(8,128)}, f32[2,256,512]{2,1,0:T(8,128)}, f32[4,128,256]{2,1,0:T(8,128)}, f32[8,256]{1,0:T(8,128)}) custom-call(s32[1]{0:T(128)} %bitcast.1.y_ref, f32[4,4,2,32,256]{4,3,2,1,0:T(8,128)} %copy-done.6, f32[4,136,256]{2,1,0:T(8,128)} %get-tuple-element.32.part_ref, f32[4,136,256]{2,1,0:T(8,128)} %copy-done.12, ...), custom_call_target="tpu_custom_call" | custom-call | flops 6442450944 | bytes 8388608 | tf_op jit(solution)/shard_map/pallas_call | solution.py:376
  126.7 2.8 %collective-permute-start.20 = (f32[2,256,512]{2,1,0:T(8,128)}, f32[2,256,512]{2,1,0:T(8,128)S(1)}, u32[]{:S(2)}, u32[]{:S(2)}) collective-permute-start(f32[2,256,512]{2,1,0:T(8,128)} %get-tuple-element.56), channel_id=1, source_target_pairs={{0,1},{1,0},{2,3},{3,2},{4,5},{5,4},{6,7},{7,6},{8,9},{9,8},{10,11... | collective-permute-start | bytes 3145736 | tf_op jit(solution)/shard_map/ppermute | solution.py:408
  130.4 12.2 %shard_map.71 = (f32[2,256,512]{2,1,0:T(8,128)}, f32[2,256,512]{2,1,0:T(8,128)}, f32[512,256]{1,0:T(8,128)}) custom-call(s32[1]{0:T(128)} %bitcast.1.y_ref, f32[4,4,2,32,256]{4,3,2,1,0:T(8,128)} %copy-done.6, f32[4,136,256]{2,1,0:T(8,128)} %get-tuple-element.38.part_ref, f32[4,136,256]{2,1,0:T(8,128)} %copy-done.7, ...), custom_call_target="tpu_custom_call" | custom-call | flops 6442450944 | bytes 8388608 | tf_op jit(solution)/shard_map/pallas_call | solution.py:376
  142.6 8.7 %shard_map.72 = (f32[1,256,512]{2,1,0:T(8,128)}, f32[1,256,512]{2,1,0:T(8,128)}, f32[512,256]{1,0:T(8,128)}) custom-call(s32[1]{0:T(128)} %bitcast.1.y_ref, f32[4,4,2,32,256]{4,3,2,1,0:T(8,128)} %copy-done.6, f32[4,136,256]{2,1,0:T(8,128)} %get-tuple-element.38.part_ref, f32[4,136,256]{2,1,0:T(8,128)} %copy-done.7, ...), custom_call_target="tpu_custom_call" | custom-call | flops 3221225472 | bytes 4194304 | tf_op jit(solution)/shard_map/pallas_call | solution.py:376
  151.3 9.1 %shard_map.75 = (f32[1,256,512]{2,1,0:T(8,128)}, f32[1,256,512]{2,1,0:T(8,128)}, f32[4,272,256]{2,1,0:T(8,128)}) custom-call(s32[1]{0:T(128)} %bitcast.1.y_ref, f32[4,4,2,32,256]{4,3,2,1,0:T(8,128)} %copy-done.6, f32[4,136,256]{2,1,0:T(8,128)} %get-tuple-element.38.part_ref, f32[4,136,256]{2,1,0:T(8,128)} %copy-done.7, ...), custom_call_target="tpu_custom_call" | custom-call | flops 3221225472 | bytes 4194304 | tf_op jit(solution)/shard_map/pallas_call | solution.py:376
  160.4 4.5 %all-to-all-start.6 = ((f32[4,272,256]{2,1,0:T(8,128)}), f32[4,272,256]{2,1,0:T(8,128)}, u32[]{:S(2)}, u32[]{:S(2)}) async-start(f32[4,272,256]{2,1,0:T(8,128)} %get-tuple-element.48), calls=%async_computation.6 | async-start | bytes 2228224 | tf_op jit(solution)/shard_map/all_to_all | solution.py:499
  167.1 2.7 %fusion.1 = (f32[256,512]{1,0:T(8,128)}, f32[256,512]{1,0:T(8,128)}) fusion(f32[2,256,512]{2,1,0:T(8,128)} %collective-permute-done.21, f32[2,256,512]{2,1,0:T(8,128)} %get-tuple-element.57), kind=kLoop, calls=%fused_computation.3 | loop fusion | flops 262144 | bytes 3145728 | tf_op jit(solution)/shard_map/add | solution.py:470
  169.8 2.7 %collective-permute-start.23 = (f32[256,512]{1,0:T(8,128)}, f32[256,512]{1,0:T(8,128)}, u32[]{:S(2)}, u32[]{:S(2)}) collective-permute-start(f32[256,512]{1,0:T(8,128)} %get-tuple-element.59), channel_id=1, source_target_pairs={{0,24},{8,0},{16,8},{24,16},{1,25},{9,1},{17,9},{25,17},{2,26},{10... | collective-permute-start | bytes 1572872 | tf_op jit(solution)/shard_map/ppermute | solution.py:407
  172.4 7.8 %all-to-all-done.6 = f32[4,272,256]{2,1,0:T(8,128)} async-done(((f32[4,272,256]{2,1,0:T(8,128)}), f32[4,272,256]{2,1,0:T(8,128)}, u32[]{:S(2)}, u32[]{:S(2)}) %all-to-all-start.6) | async-done | bytes 1114144 | tf_op jit(solution)/shard_map/all_to_all | solution.py:499
  182.4 5.1 %all-to-all-start.7 = ((f32[4,80,256]{2,1,0:T(8,128)}), f32[4,80,256]{2,1,0:T(8,128)S(1)}, u32[]{:S(2)}, u32[]{:S(2)}) async-start(f32[4,80,256]{2,1,0:T(8,128)} %pad_maximum_fusion), calls=%async_computation.7 | async-start | bytes 655360 | tf_op jit(solution)/shard_map/all_to_all | solution.py:504
  189.9 3.5 %all-to-all-done.7.slots_ref = f32[4,80,256]{2,1,0:T(8,128)S(1)} async-done(((f32[4,80,256]{2,1,0:T(8,128)}), f32[4,80,256]{2,1,0:T(8,128)S(1)}, u32[]{:S(2)}, u32[]{:S(2)}) %all-to-all-start.7) | async-done | bytes 327712 | tf_op jit(solution)/shard_map/all_to_all | solution.py:504
  193.4 3.1 %collective-permute-start.25 = (f32[64,256]{1,0:T(8,128)S(1)}, f32[64,256]{1,0:T(8,128)S(1)}, u32[]{:S(2)}, u32[]{:S(2)}) collective-permute-start(f32[64,256]{1,0:T(8,128)S(1)} %bitcast.35), channel_id=1, source_target_pairs={{0,1},{1,0},{2,3},{3,2},{4,5},{5,4},{6,7},{7,6},{8,9},{9,8},{10,11... | collective-permute-start | bytes 196616 | tf_op jit(solution)/shard_map/ppermute | solution.py:408
  198.3 2.7 %collective-permute-start.17 = (f32[256,512]{1,0:T(8,128)S(1)}, f32[256,512]{1,0:T(8,128)S(1)}, u32[]{:S(2)}, u32[]{:S(2)}) collective-permute-start(f32[256,512]{1,0:T(8,128)S(1)} %get-tuple-element.61), channel_id=1, source_target_pairs={{0,24},{8,0},{16,8},{24,16},{1,25},{9,1},{17,9},{25,17},{2,26},{10... | collective-permute-start | bytes 1572872 | tf_op jit(solution)/shard_map/ppermute | solution.py:407
  202.4 22.5 %collective-permute-done.28 = f32[64,256]{1,0:T(8,128)S(1)} collective-permute-done((f32[64,256]{1,0:T(8,128)S(1)}, f32[64,256]{1,0:T(8,128)S(1)}, u32[]{:S(2)}, u32[]{:S(2)}) %collective-permute-start.28) | collective-permute-done | bytes 65568 | tf_op jit(solution)/shard_map/ppermute | solution.py:407
  225.7 4.0 %collective-permute-done.27 = f32[64,256]{1,0:T(8,128)S(1)} collective-permute-done((f32[64,256]{1,0:T(8,128)S(1)}, f32[64,256]{1,0:T(8,128)S(1)}, u32[]{:S(2)}, u32[]{:S(2)}) %collective-permute-start.27) | collective-permute-done | bytes 65568 | tf_op jit(solution)/shard_map/ppermute | solution.py:407
  230.5 2.2 shard_map.76.refs_0_
  (104 shorter events, 30.3 us)
Async XLA Ops:
  1.9 27.3 %collective-permute-start.7 = (f32[512,256]{1,0:T(8,128)S(1)}, f32[512,256]{1,0:T(8,128)S(1)}, u32[]{:S(2)}, u32[]{:S(2)}) collective-permute-start(f32[512,256]{1,0:T(8,128)S(1)} %get-tuple-element.63.refs_6_), channel_id=1, source_target_pairs={{0,24},{8,0},{16,8},{24,16},{1,25},{9,1},{17,9},{25,17},{2,26},{10... | collective-permute-start | bytes 1572872 | tf_op jit(solution)/shard_map/ppermute | solution.py:407
  5.3 24.1 %collective-permute-start.5 = (f32[512,256]{1,0:T(8,128)S(1)}, f32[512,256]{1,0:T(8,128)}, u32[]{:S(2)}, u32[]{:S(2)}) collective-permute-start(f32[512,256]{1,0:T(8,128)S(1)} %get-tuple-element.63.refs_6_), channel_id=1, source_target_pairs={{0,8},{8,16},{16,24},{24,0},{1,9},{9,17},{17,25},{25,1},{2,10},{10... | collective-permute-start | bytes 1572872 | tf_op jit(solution)/shard_map/ppermute | solution.py:407
  5.3 26.9 %collective-permute-start.3 = (f32[512,256]{1,0:T(8,128)S(1)}, f32[512,256]{1,0:T(8,128)}, u32[]{:S(2)}, u32[]{:S(2)}) collective-permute-start(f32[512,256]{1,0:T(8,128)S(1)} %get-tuple-element.63.refs_6_), channel_id=1, source_target_pairs={{0,16},{8,24},{16,0},{24,8},{1,17},{9,25},{17,1},{25,9},{2,18},{10... | collective-permute-start | bytes 1572872 | tf_op jit(solution)/shard_map/ppermute | solution.py:407
  22.2 16.6 %all-to-all-start.1 = ((f32[4,4,2,32,256]{4,3,2,1,0:T(8,128)}), f32[4,4,2,32,256]{4,3,2,1,0:T(8,128)S(1)}, u32[]{:S(2)}, u32[]{:S(2)}) async-start(f32[4,4,2,32,256]{4,3,2,1,0:T(8,128)} %broadcast_in_dim.4), calls=%async_computation.1 | async-start | bytes 2097152 | tf_op jit(solution)/shard_map/all_to_all | solution.py:430
  29.4 9.4 %collective-permute-start.6 = (f32[512,256]{1,0:T(8,128)}, f32[512,256]{1,0:T(8,128)}, u32[]{:S(2)}, u32[]{:S(2)}) collective-permute-start(f32[512,256]{1,0:T(8,128)} %collective-permute-done.5.refs_2_), channel_id=1, source_target_pairs={{0,1},{1,0},{2,3},{3,2},{4,5},{5,4},{6,7},{7,6},{8,9},{9,8},{10,11... | collective-permute-start | bytes 1572872 | tf_op jit(solution)/shard_map/ppermute | solution.py:408
  32.2 6.6 %collective-permute-start.4 = (f32[512,256]{1,0:T(8,128)}, f32[512,256]{1,0:T(8,128)}, u32[]{:S(2)}, u32[]{:S(2)}) collective-permute-start(f32[512,256]{1,0:T(8,128)} %collective-permute-done.3.refs_0_), channel_id=1, source_target_pairs={{0,1},{1,0},{2,3},{3,2},{4,5},{5,4},{6,7},{7,6},{8,9},{9,8},{10,11... | collective-permute-start | bytes 1572872 | tf_op jit(solution)/shard_map/ppermute | solution.py:408
  32.2 21.6 %collective-permute-start.2 = (f32[512,256]{1,0:T(8,128)S(1)}, f32[512,256]{1,0:T(8,128)S(1)}, u32[]{:S(2)}, u32[]{:S(2)}) collective-permute-start(f32[512,256]{1,0:T(8,128)S(1)} %get-tuple-element.36.refs_6_), channel_id=1, source_target_pairs={{0,16},{8,24},{16,0},{24,8},{1,17},{9,25},{17,1},{25,9},{2,18},{10... | collective-permute-start | bytes 1572872 | tf_op jit(solution)/shard_map/ppermute | solution.py:407
  32.5 23.9 %collective-permute-start.1 = (f32[512,256]{1,0:T(8,128)S(1)}, f32[512,256]{1,0:T(8,128)S(1)}, u32[]{:S(2)}, u32[]{:S(2)}) collective-permute-start(f32[512,256]{1,0:T(8,128)S(1)} %get-tuple-element.36.refs_6_), channel_id=1, source_target_pairs={{0,24},{8,0},{16,8},{24,16},{1,25},{9,1},{17,9},{25,17},{2,26},{10... | collective-permute-start | bytes 1572872 | tf_op jit(solution)/shard_map/ppermute | solution.py:407
  34.7 24.1 %collective-permute-start = (f32[512,256]{1,0:T(8,128)S(1)}, f32[512,256]{1,0:T(8,128)S(1)}, u32[]{:S(2)}, u32[]{:S(2)}) collective-permute-start(f32[512,256]{1,0:T(8,128)S(1)} %get-tuple-element.36.refs_6_), channel_id=1, source_target_pairs={{0,8},{8,16},{16,24},{24,0},{1,9},{9,17},{17,25},{25,1},{2,10},{10... | collective-permute-start | bytes 1572872 | tf_op jit(solution)/shard_map/ppermute | solution.py:407
  58.8 19.2 %collective-permute-start.10 = (f32[512,256]{1,0:T(8,128)S(1)}, f32[512,256]{1,0:T(8,128)}, u32[]{:S(2)}, u32[]{:S(2)}) collective-permute-start(f32[512,256]{1,0:T(8,128)S(1)} %collective-permute-done.2.refs_0_), channel_id=1, source_target_pairs={{0,1},{1,0},{2,3},{3,2},{4,5},{5,4},{6,7},{7,6},{8,9},{9,8},{10,11... | collective-permute-start | bytes 1572872 | tf_op jit(solution)/shard_map/ppermute | solution.py:408
  59.3 18.8 %collective-permute-start.11 = (f32[512,256]{1,0:T(8,128)S(1)}, f32[512,256]{1,0:T(8,128)}, u32[]{:S(2)}, u32[]{:S(2)}) collective-permute-start(f32[512,256]{1,0:T(8,128)S(1)} %collective-permute-done.refs_2_), channel_id=1, source_target_pairs={{0,1},{1,0},{2,3},{3,2},{4,5},{5,4},{6,7},{7,6},{8,9},{9,8},{10,11... | collective-permute-start | bytes 1572872 | tf_op jit(solution)/shard_map/ppermute | solution.py:408
  59.3 18.8 %collective-permute-start.12 = (f32[512,256]{1,0:T(8,128)S(1)}, f32[512,256]{1,0:T(8,128)}, u32[]{:S(2)}, u32[]{:S(2)}) collective-permute-start(f32[512,256]{1,0:T(8,128)S(1)} %collective-permute-done.1.refs_4_), channel_id=1, source_target_pairs={{0,1},{1,0},{2,3},{3,2},{4,5},{5,4},{6,7},{7,6},{8,9},{9,8},{10,11... | collective-permute-start | bytes 1572872 | tf_op jit(solution)/shard_map/ppermute | solution.py:408
  59.8 18.3 %collective-permute-start.13 = (f32[512,256]{1,0:T(8,128)S(1)}, f32[512,256]{1,0:T(8,128)}, u32[]{:S(2)}, u32[]{:S(2)}) collective-permute-start(f32[512,256]{1,0:T(8,128)S(1)} %get-tuple-element.36.refs_6_), channel_id=1, source_target_pairs={{0,1},{1,0},{2,3},{3,2},{4,5},{5,4},{6,7},{7,6},{8,9},{9,8},{10,11... | collective-permute-start | bytes 1572872 | tf_op jit(solution)/shard_map/ppermute | solution.py:408
  59.8 13.3 %all-to-all-start.2 = ((f32[4,136,256]{2,1,0:T(8,128)}), f32[4,136,256]{2,1,0:T(8,128)S(1)}, u32[]{:S(2)}, u32[]{:S(2)}) async-start(f32[4,136,256]{2,1,0:T(8,128)} %get-tuple-element.32.part_ref), calls=%async_computation.2 | async-start | bytes 1114112 | tf_op jit(solution)/shard_map/all_to_all | solution.py:446
  74.5 17.6 %all-to-all-start.3 = ((f32[4,136,256]{2,1,0:T(8,128)}), f32[4,136,256]{2,1,0:T(8,128)S(1)}, u32[]{:S(2)}, u32[]{:S(2)}) async-start(f32[4,136,256]{2,1,0:T(8,128)} %shard_map.69), calls=%async_computation.3 | async-start | bytes 1114112 | tf_op jit(solution)/shard_map/all_to_all | solution.py:458
  92.1 16.5 %all-to-all-start.4 = ((f32[4,136,256]{2,1,0:T(8,128)}), f32[4,136,256]{2,1,0:T(8,128)S(1)}, u32[]{:S(2)}, u32[]{:S(2)}) async-start(f32[4,136,256]{2,1,0:T(8,128)} %get-tuple-element.38.part_ref), calls=%async_computation.4 | async-start | bytes 1114112 | tf_op jit(solution)/shard_map/all_to_all | solution.py:446
  110.0 19.6 %all-to-all-start.5 = ((f32[4,136,256]{2,1,0:T(8,128)}), f32[4,136,256]{2,1,0:T(8,128)S(1)}, u32[]{:S(2)}, u32[]{:S(2)}) async-start(f32[4,136,256]{2,1,0:T(8,128)} %shard_map.70), calls=%async_computation.5 | async-start | bytes 1114112 | tf_op jit(solution)/shard_map/all_to_all | solution.py:458
  126.7 39.5 %collective-permute-start.20 = (f32[2,256,512]{2,1,0:T(8,128)}, f32[2,256,512]{2,1,0:T(8,128)S(1)}, u32[]{:S(2)}, u32[]{:S(2)}) collective-permute-start(f32[2,256,512]{2,1,0:T(8,128)} %get-tuple-element.56), channel_id=1, source_target_pairs={{0,1},{1,0},{2,3},{3,2},{4,5},{5,4},{6,7},{7,6},{8,9},{9,8},{10,11... | collective-permute-start | bytes 3145736 | tf_op jit(solution)/shard_map/ppermute | solution.py:408
  129.5 37.6 %collective-permute-start.21 = (f32[2,256,512]{2,1,0:T(8,128)}, f32[2,256,512]{2,1,0:T(8,128)}, u32[]{:S(2)}, u32[]{:S(2)}) collective-permute-start(f32[2,256,512]{2,1,0:T(8,128)} %get-tuple-element.58), channel_id=1, source_target_pairs={{0,1},{1,0},{2,3},{3,2},{4,5},{5,4},{6,7},{7,6},{8,9},{9,8},{10,11... | collective-permute-start | bytes 3145736 | tf_op jit(solution)/shard_map/ppermute | solution.py:408
  160.4 19.8 %all-to-all-start.6 = ((f32[4,272,256]{2,1,0:T(8,128)}), f32[4,272,256]{2,1,0:T(8,128)}, u32[]{:S(2)}, u32[]{:S(2)}) async-start(f32[4,272,256]{2,1,0:T(8,128)} %get-tuple-element.48), calls=%async_computation.6 | async-start | bytes 2228224 | tf_op jit(solution)/shard_map/all_to_all | solution.py:499
  165.0 28.4 %collective-permute-start.15 = (f32[2,256,512]{2,1,0:T(8,128)}, f32[2,256,512]{2,1,0:T(8,128)}, u32[]{:S(2)}, u32[]{:S(2)}) collective-permute-start(f32[2,256,512]{2,1,0:T(8,128)} %get-tuple-element.52), channel_id=1, source_target_pairs={{0,1},{1,0},{2,3},{3,2},{4,5},{5,4},{6,7},{7,6},{8,9},{9,8},{10,11... | collective-permute-start | bytes 3145736 | tf_op jit(solution)/shard_map/ppermute | solution.py:408
  165.7 69.3 %collective-permute-start.14 = (f32[1,256,512]{2,1,0:T(8,128)}, f32[1,256,512]{2,1,0:T(8,128)S(1)}, u32[]{:S(2)}, u32[]{:S(2)}) collective-permute-start(f32[1,256,512]{2,1,0:T(8,128)} %get-tuple-element.50), channel_id=1, source_target_pairs={{0,1},{1,0},{2,3},{3,2},{4,5},{5,4},{6,7},{7,6},{8,9},{9,8},{10,11... | collective-permute-start | bytes 1572872 | tf_op jit(solution)/shard_map/ppermute | solution.py:408
  165.7 21.8 %collective-permute-start.18 = (f32[1,256,512]{2,1,0:T(8,128)}, f32[1,256,512]{2,1,0:T(8,128)}, u32[]{:S(2)}, u32[]{:S(2)}) collective-permute-start(f32[1,256,512]{2,1,0:T(8,128)} %get-tuple-element.54), channel_id=1, source_target_pairs={{0,1},{1,0},{2,3},{3,2},{4,5},{5,4},{6,7},{7,6},{8,9},{9,8},{10,11... | collective-permute-start | bytes 1572872 | tf_op jit(solution)/shard_map/ppermute | solution.py:408
  167.1 31.2 %collective-permute-start.24 = (f32[256,512]{1,0:T(8,128)}, f32[256,512]{1,0:T(8,128)S(1)}, u32[]{:S(2)}, u32[]{:S(2)}) collective-permute-start(f32[256,512]{1,0:T(8,128)} %fusion), channel_id=1, source_target_pairs={{0,8},{8,16},{16,24},{24,0},{1,9},{9,17},{17,25},{25,1},{2,10},{10... | collective-permute-start | bytes 1572872 | tf_op jit(solution)/shard_map/ppermute | solution.py:407
  169.8 28.6 %collective-permute-start.23 = (f32[256,512]{1,0:T(8,128)}, f32[256,512]{1,0:T(8,128)}, u32[]{:S(2)}, u32[]{:S(2)}) collective-permute-start(f32[256,512]{1,0:T(8,128)} %get-tuple-element.59), channel_id=1, source_target_pairs={{0,24},{8,0},{16,8},{24,16},{1,25},{9,1},{17,9},{25,17},{2,26},{10... | collective-permute-start | bytes 1572872 | tf_op jit(solution)/shard_map/ppermute | solution.py:407
  182.4 10.9 %all-to-all-start.7 = ((f32[4,80,256]{2,1,0:T(8,128)}), f32[4,80,256]{2,1,0:T(8,128)S(1)}, u32[]{:S(2)}, u32[]{:S(2)}) async-start(f32[4,80,256]{2,1,0:T(8,128)} %pad_maximum_fusion), calls=%async_computation.7 | async-start | bytes 655360 | tf_op jit(solution)/shard_map/all_to_all | solution.py:504
  187.5 13.5 %collective-permute-start.22 = (f32[256,512]{1,0:T(8,128)}, f32[256,512]{1,0:T(8,128)}, u32[]{:S(2)}, u32[]{:S(2)}) collective-permute-start(f32[256,512]{1,0:T(8,128)} %get-tuple-element.60), channel_id=1, source_target_pairs={{0,16},{8,24},{16,0},{24,8},{1,17},{9,25},{17,1},{25,9},{2,18},{10... | collective-permute-start | bytes 1572872 | tf_op jit(solution)/shard_map/ppermute | solution.py:407
  193.4 7.6 %collective-permute-start.25 = (f32[64,256]{1,0:T(8,128)S(1)}, f32[64,256]{1,0:T(8,128)S(1)}, u32[]{:S(2)}, u32[]{:S(2)}) collective-permute-start(f32[64,256]{1,0:T(8,128)S(1)} %bitcast.35), channel_id=1, source_target_pairs={{0,1},{1,0},{2,3},{3,2},{4,5},{5,4},{6,7},{7,6},{8,9},{9,8},{10,11... | collective-permute-start | bytes 196616 | tf_op jit(solution)/shard_map/ppermute | solution.py:408
  198.2 36.7 %collective-permute-start.19 = (f32[256,512]{1,0:T(8,128)}, f32[256,512]{1,0:T(8,128)S(1)}, u32[]{:S(2)}, u32[]{:S(2)}) collective-permute-start(f32[256,512]{1,0:T(8,128)} %add_bitcast_fusion), channel_id=1, source_target_pairs={{0,8},{8,16},{16,24},{24,0},{1,9},{9,17},{17,25},{25,1},{2,10},{10... | collective-permute-start | bytes 1572872 | tf_op jit(solution)/shard_map/ppermute | solution.py:407
  198.3 36.6 %collective-permute-start.17 = (f32[256,512]{1,0:T(8,128)S(1)}, f32[256,512]{1,0:T(8,128)S(1)}, u32[]{:S(2)}, u32[]{:S(2)}) collective-permute-start(f32[256,512]{1,0:T(8,128)S(1)} %get-tuple-element.61), channel_id=1, source_target_pairs={{0,24},{8,0},{16,8},{24,16},{1,25},{9,1},{17,9},{25,17},{2,26},{10... | collective-permute-start | bytes 1572872 | tf_op jit(solution)/shard_map/ppermute | solution.py:407
  201.0 34.0 %collective-permute-start.16 = (f32[256,512]{1,0:T(8,128)S(1)}, f32[256,512]{1,0:T(8,128)S(1)}, u32[]{:S(2)}, u32[]{:S(2)}) collective-permute-start(f32[256,512]{1,0:T(8,128)S(1)} %get-tuple-element.62), channel_id=1, source_target_pairs={{0,16},{8,24},{16,0},{24,8},{1,17},{9,25},{17,1},{25,9},{2,18},{10... | collective-permute-start | bytes 1572872 | tf_op jit(solution)/shard_map/ppermute | solution.py:407
  201.0 23.9 %collective-permute-start.28 = (f32[64,256]{1,0:T(8,128)S(1)}, f32[64,256]{1,0:T(8,128)S(1)}, u32[]{:S(2)}, u32[]{:S(2)}) collective-permute-start(f32[64,256]{1,0:T(8,128)S(1)} %bitcast_add_fusion), channel_id=1, source_target_pairs={{0,24},{8,0},{16,8},{24,16},{1,25},{9,1},{17,9},{25,17},{2,26},{10... | collective-permute-start | bytes 196616 | tf_op jit(solution)/shard_map/ppermute | solution.py:407
  (21 other events, 285.3 us)
